TPU v7x, 128 devices: a whole 4x4x4 slice. The times are simulated.
128 devices in a mesh: row: 8 (over z, y_lo), col: 16 (over y_hi, x, core).
Axes of the slice: x: 4, y: 4 (y_hi: 2, y_lo: 2; y = y_hi * 2 + y_lo), z: 4, core: 2. Of those that a mesh axis runs over, the one named last changes fastest.
Arguments:
- stiffness: float32 [4, 8, 512, 2, 16, 512], P(None, 'row', None, None, 'col'), may hold values from -7 to 7
- lower_panel: float32 [4, 8, 512, 512], P(None, 'row'), may hold values from -0.25 to 0.25
- diag_inverse: float32 [512, 512], replicated, as said below
Outputs:
- reduced: float32 [4, 8, 512, 2, 16, 512], P(None, 'row', None, None, 'col')
Inputs may be any that keep to these rules, and one draw needn't show every extreme that they name: diag_inverse is lower triangular with a positive diagonal.
All inputs are finite; a program needn't handle non-finite values.
Results may differ from a plain program's by a relative error of at most 0.000062.
Values sent between devices are 32-bit elements; how exact they have to be, the bound alone decides.
A program may use at most 128 MiB of HBM per device.

v0:
```python
import jax
import jax.numpy as jnp
from jax import lax
from jax.sharding import PartitionSpec as P


def spread(value, axis, source):
    kept = jnp.where(lax.axis_index(axis) == source, value, 0).astype(value.dtype)
    return lax.psum(kept, axis)


def body(stiffness, lower_panel, diag_inverse):
    highest = lax.Precision.HIGHEST
    rows = lax.axis_size("row")
    cols = lax.axis_size("col")
    my_row = lax.axis_index("row")
    my_col = lax.axis_index("col")
    blocks = stiffness[:, 0, :, :, 0, :]
    brows = blocks.shape[0]
    width = blocks.shape[1]
    bcols = blocks.shape[2]
    row_ids = jnp.arange(brows) * rows + my_row
    keep_rows = (row_ids != 0)[:, None, None]
    lower_rows = jnp.where(keep_rows, lower_panel[:, 0], 0.0)
    column_zero = spread(blocks[:, :, 0, :], "col", 0)
    corner_source = column_zero[0]
    corner = spread(corner_source, "row", 0)
    c_block = jnp.dot(
        jnp.dot(diag_inverse, corner, precision=highest), diag_inverse.T, precision=highest
    )
    panel_rows = jnp.where(keep_rows, column_zero, 0.0)
    lower_c_rows = jnp.einsum("bik,kj->bij", lower_rows, c_block, precision=highest)
    w_rows = (
        jnp.einsum("bik,jk->bij", panel_rows, diag_inverse, precision=highest) - 0.5 * lower_c_rows
    )
    final_rows = w_rows - 0.5 * lower_c_rows
    ratio = cols // rows
    source = my_col % rows
    offset = my_col // rows
    values = jnp.concatenate([w_rows, lower_rows], axis=2)
    grouped = values.reshape(bcols, ratio, width, values.shape[-1])
    joined = spread(lax.dynamic_index_in_dim(grouped, offset, 1, keepdims=False), "row", source)
    w_cols = joined[:, :, :width]
    lower_cols = joined[:, :, width:]
    lower_c_cols = jnp.einsum("bik,kj->bij", lower_cols, c_block, precision=highest)
    update = blocks - jnp.einsum("bik,cjk->bicj", w_rows, lower_cols, precision=highest)
    update = update - jnp.einsum("bik,cjk->bicj", lower_rows, w_cols, precision=highest)
    final_cols = w_cols - 0.5 * lower_c_cols
    first_column = jnp.where(my_col == 0, final_rows, update[:, :, 0, :])
    update = update.at[:, :, 0, :].set(first_column)
    first_row = jnp.where(my_row == 0, jnp.transpose(final_cols, (2, 0, 1)), update[0])
    update = update.at[0].set(first_row)
    at_corner = jnp.logical_and(my_row == 0, my_col == 0)
    update = update.at[0, :, 0, :].set(jnp.where(at_corner, c_block, update[0, :, 0, :]))
    return update[:, None, :, :, None, :]


def solution(mesh):
    in_specs = (P(None, "row", None, None, "col", None), P(None, "row", None, None), P())
    out_specs = P(None, "row", None, None, "col", None)
    return jax.shard_map(body, mesh=mesh, in_specs=in_specs, out_specs=out_specs, check_vma=False)
```

profile of v0, /device:TPU:1, one launch (start us, length us, event | category | flops | bytes accessed | tf_op | source)
XLA Modules:
  0.0 576.5 jit_solution(12848044044958805449)
XLA Ops:
  6.5 0.0 copy-start
  6.5 0.0 all-reduce.4.cloned.1.call-start
  6.5 20.6 %copy.17 = f32[4,1,512,2,1,512]{2,5,0,3,4,1:T(8,128)} copy(f32[4,1,512,2,1,512]{5,4,3,2,1,0:T(1,128)} %param.9) | data formatting | bytes 16777216 | tf_op args[0]
  27.1 4.7 fusion.3
  31.8 0.0 all-reduce.4.cloned.1.call-update
  31.8 0.0 all-reduce.6.cloned.1.call-start
  31.9 153.0 %all-reduce.4.cloned.1.call-done = f32[4,512,512]{1,2,0:T(8,128)} async-done(((f32[4,512,512]{1,2,0:T(8,128)}), f32[4,512,512]{1,2,0:T(8,128)}) %all-reduce.4.cloned.1.call-update) | async-done | bytes 4194320 | tf_op jit(solution)/shard_map/psum | solution.py:9
  184.9 2.3 fusion.28
  187.2 0.0 all-reduce.6.cloned.1.call-update
  187.2 0.0 all-reduce.8.cloned.1.call-start
  187.3 5.3 copy.19
  192.6 4.8 bitcast_select_fusion
  197.3 68.0 %all-reduce.6.cloned.1.call-done = f32[512,512]{0,1:T(8,128)} async-done(((f32[512,512]{0,1:T(8,128)}), f32[512,512]{0,1:T(8,128)}) %all-reduce.6.cloned.1.call-update) | async-done | bytes 1048592 | tf_op jit(solution)/shard_map/psum | solution.py:9
  265.4 0.0 copy-done
  265.4 0.0 copy-start.2
  265.4 3.2 fusion.34
  268.6 3.5 fusion.35
  272.1 0.0 copy-done.2
  272.1 0.0 copy-start.8
  272.1 8.5 %fusion.30 = f32[4,512,512]{1,2,0:T(8,128)S(1)} fusion(f32[4,512,512]{1,2,0:T(8,128)S(1)} %copy-done.2, f32[512,512]{1,0:T(8,128)S(1)} %fusion.35), kind=kOutput, calls=%fused_computation.35 | convolution fusion | flops 6442450944 | bytes 9437184 | tf_op jit(solution)/shard_map/bik,kj->bij/dot_general | solution.py:32
  280.7 0.0 copy-start.5
  280.7 2.0 copy-done.5
  282.6 0.0 copy-done.8
  282.6 8.6 %multiply_subtract_fusion = f32[4,512,512]{1,2,0:T(8,128)S(1)} fusion(f32[4,512,512]{1,2,0:T(8,128)S(1)} %fusion.30, f32[4,512,512]{1,2,0:T(8,128)S(1)} %copy-done.8, pred[4]{0:T(512)(128)(4,1)S(1)} %add_compare_fusion, f32[512,512]{1,0:T(8,128)S(1)} %copy-done), kind=kOutput, calls=%fused_computation.16 | convolution fusion | flops 6445596672 | bytes 13631492 | tf_op jit(solution)/shard_map/bik,jk->bij/dot_general | solution.py:34
  291.3 0.0 copy-start.3
  291.3 4.5 pad_maximum_fusion
  295.7 0.0 copy-done.3
  295.7 4.6 constant_dynamic-slice_fusion
  300.3 5.6 copy.46
  305.9 2.8 select_bitcast_fusion
  308.7 0.0 all-reduce.8.cloned.1.call-update
  308.7 0.3 copy.29
  309.0 187.5 %all-reduce.8.cloned.1.call-done = f32[2,512,1024]{2,1,0:T(8,128)} async-done(((f32[2,512,1024]{2,1,0:T(8,128)}), f32[2,512,1024]{2,1,0:T(8,128)}) %all-reduce.8.cloned.1.call-update) | async-done | bytes 4194320 | tf_op jit(solution)/shard_map/psum | solution.py:9
  496.6 0.0 copy-start.4
  496.6 18.6 %fusion.4 = f32[4,512,2,512]{1,3,0,2:T(8,128)} fusion(f32[4,512,512]{1,2,0:T(8,128)} %bitcast_select_fusion, f32[2,512,1024]{2,1,0:T(8,128)} %all-reduce.8.cloned.1.call-done), kind=kOutput, calls=%fused_computation.8 | convolution fusion | flops 12884901888 | bytes 14680064 | tf_op jit(solution)/shard_map/bik,cjk->bicj/dot_general | solution.py:47
  515.2 0.0 copy-done.4
  515.2 0.0 copy-start.6
  515.2 20.5 %subtract_subtract_fusion = f32[4,512,2,512]{1,3,0,2:T(8,128)S(1)} fusion(f32[4,512,2,512]{1,3,0,2:T(8,128)} %fusion.4, f32[4,512,512]{1,2,0:T(8,128)S(1)} %copy-done.4, f32[2,512,1024]{2,1,0:T(8,128)} %all-reduce.8.cloned.1.call-done, f32[4,1,512,2,1,512]{2,5,0,3,4,1:T(8,128)} %copy.17), kind=kOutput, calls=%fused_computation.1 | convolution fusion | flops 12889096192 | bytes 31457280 | tf_op jit(solution)/shard_map/bik,cjk->bicj/dot_general | solution.py:46
  535.7 0.0 copy-done.6
  535.7 2.2 fusion.2
  537.9 0.0 copy-start.7
  537.9 4.3 copy.51
  542.2 1.0 copy-done.7
  543.1 4.9 bitcast_dynamic-update-slice_fusion
  548.1 0.0 copy-start.1
  548.1 1.2 fusion.27
  549.3 20.5 %copy.31 = f32[4,1,512,2,1,512]{5,4,3,2,1,0:T(1,128)} copy(f32[4,1,512,2,1,512]{2,5,0,3,4,1:T(8,128)} %fusion.27) | data formatting | bytes 16777216 | tf_op jit(solution)/shard_map/scatter | solution.py:54
  569.8 0.0 copy-done.1
  (1 shorter events, 0.0 us)
Async XLA Ops:
  6.5 258.8 %copy-start = (f32[512,512]{1,0:T(8,128)S(1)}, f32[512,512]{1,0:T(8,128)}, u32[]{:S(2)}) copy-start(f32[512,512]{1,0:T(8,128)} %param.11) | copy-start | bytes 3145732
  6.5 178.3 %all-reduce.4.cloned.1.call-start = ((), (), s32[]{:S(2)}) async-start(), calls=%async_computation | async-start | bytes 8388608 | tf_op jit(solution)/shard_map/psum | solution.py:9
  31.8 233.5 %all-reduce.6.cloned.1.call-start = ((), (), s32[]{:S(2)}) async-start(), calls=%async_computation.1 | async-start | bytes 2097152 | tf_op jit(solution)/shard_map/psum | solution.py:9
  187.2 309.4 %all-reduce.8.cloned.1.call-start = ((), (), s32[]{:S(2)}) async-start(), calls=%async_computation.2 | async-start | bytes 8388608 | tf_op jit(solution)/shard_map/psum | solution.py:9
  265.4 6.7 %copy-start.2 = (f32[4,512,512]{1,2,0:T(8,128)S(1)}, f32[4,512,512]{1,2,0:T(8,128)}, u32[]{:S(2)}) copy-start(f32[4,512,512]{1,2,0:T(8,128)} %bitcast_select_fusion) | copy-start | bytes 12582916
  272.1 10.5 %copy-start.8 = (f32[4,512,512]{1,2,0:T(8,128)S(1)}, f32[4,512,512]{1,2,0:T(8,128)}, u32[]{:S(2)}) copy-start(f32[4,512,512]{1,2,0:T(8,128)} %all-reduce.4.cloned.1.call-done) | copy-start | bytes 12582916
  280.7 2.0 copy-start.5
  291.3 4.5 copy-start.3
  496.6 18.6 %copy-start.4 = (f32[4,512,512]{1,2,0:T(8,128)S(1)}, f32[4,512,512]{1,2,0:T(8,128)}, u32[]{:S(2)}) copy-start(f32[4,512,512]{1,2,0:T(8,128)} %copy-done.3) | copy-start | bytes 12582916
  515.2 20.6 %copy-start.6 = (f32[4,512,512]{1,2,0:T(8,128)S(1)}, f32[4,512,512]{1,2,0:T(8,128)}, u32[]{:S(2)}) copy-start(f32[4,512,512]{1,2,0:T(8,128)} %copy-done.5) | copy-start | bytes 12582916
  537.9 5.2 copy-start.7
  548.1 21.7 %copy-start.1 = (f32[512,512]{1,0:T(8,128)S(1)}, f32[512,512]{1,0:T(8,128)}, u32[]{:S(2)}) copy-start(f32[512,512]{1,0:T(8,128)} %param.11) | copy-start | bytes 3145732
Sparse Core Ops, SparseCore 0:
  31.9 152.8 all-reduce.3
  187.4 77.9 all-reduce.5
  308.8 187.7 all-reduce.7
where the time goes:
time: 587 us; the launch traced here: 577 us
  waiting for transfers between devices  409 us (70%)
  matrix products  67.9 us (12%)
  local copies, waits for them, and re-layouts  64.1 us (11%)
  other arithmetic  22.3 us (4%)
  between operations  13.5 us (2%)
    psum x3, waiting for transfers between devices, spread(): return lax.psum(kept, axis)  409 us
    unnamed x22, local copies, waits for them, and re-layouts  38.6 us
    dot_general x1, matrix products, body(): jnp.einsum('bik,cjk->bicj', w_rows, lower_cols, precision=highest)  20.5 us
    scatter x1, local copies, waits for them, and re-layouts, body(): update.at[0, :, 0, :].set(jnp.where(at_corner, c_block, update[0, :, 0, :]))  20.5 us
    dot_general x1, matrix products, body(): jnp.einsum('bik,cjk->bicj', lower_rows, w_cols, precision=highest)  18.6 us
  transfers between devices with their start and end apart: 3, of which 3 were waited for; matrix products, arithmetic and copies ran while one was open for 2% of the time, Pallas kernels for 0%

commit v1 on v0

--- a/solution.py
+++ b/solution.py
@@ -6,7 +6,7 @@
 
 def spread(value, axis, source):
     kept = jnp.where(lax.axis_index(axis) == source, value, 0).astype(value.dtype)
-    return lax.psum(kept, axis)
+    return jnp.sum(lax.all_gather(kept, axis), axis=0)
 
 
 def body(stiffness, lower_panel, diag_inverse):

time: 587 us -> 1360 us (2.32)
  waiting for transfers between devices: 409 us -> 1140 us
  other arithmetic: 22.3 us -> 63.1 us
    all_gather x0 -> x3, waiting for transfers between devices: none -> 1140 us  [spread(): return jnp.sum(lax.all_gather(kept, axis), axis=0)]
    psum x3 -> x0, waiting for transfers between devices: 409 us -> none  [spread(): return lax.psum(kept, axis)]
    reduce_sum x0 -> x2, other arithmetic: none -> 36.1 us  [spread(): return jnp.sum(lax.all_gather(kept, axis), axis=0)]
    unnamed x22 -> x26, local copies, waits for them, and re-layouts: 38.6 us -> 40.5 us
  transfers between devices with their start and end apart: 3 -> 3, of which waited for: 3 -> 3; matrix products, arithmetic and copies ran while one was open for 2% -> 1% of each run, Pallas kernels for 0% -> 0%
where the time goes in v1:
time: 1360 us
  waiting for transfers between devices  1140 us (84%)
  local copies, waits for them, and re-layouts  77 us (6%)
  matrix products  65.7 us (5%)
  other arithmetic  63.1 us (5%)
  between operations  13.6 us (1%)
    all_gather x3, waiting for transfers between devices, spread(): return jnp.sum(lax.all_gather(kept, axis), axis=0)  1140 us
    unnamed x26, local copies, waits for them, and re-layouts  40.5 us
    reduce_sum x2, other arithmetic, spread(): return jnp.sum(lax.all_gather(kept, axis), axis=0)  36.1 us
  transfers between devices with their start and end apart: 3, of which 3 were waited for; matrix products, arithmetic and copies ran while one was open for 1% of the time, Pallas kernels for 0%

profile of v1, /device:TPU:1, one launch (start us, length us, event | category | flops | bytes accessed | tf_op | source)
XLA Modules:
  0.0 1358.1 jit_solution(13993571044760873278)
XLA Ops:
  6.5 0.0 copy-start
  6.5 0.0 all-gather.8.cloned.1.call-start
  6.5 20.6 %copy.37 = f32[4,1,512,2,1,512]{2,5,0,3,4,1:T(8,128)} copy(f32[4,1,512,2,1,512]{5,4,3,2,1,0:T(1,128)} %param.9) | data formatting | bytes 16777216 | tf_op args[0]
  27.1 4.6 slice_select_fusion
  31.8 5.2 copy.38
  37.0 0.0 all-gather.8.cloned.1.call-update
  37.1 0.0 all-gather.6.cloned.1.call-start
  37.1 346.2 %all-gather.8.cloned.1.call-done = f32[64,512,1,512]{3,1,2,0:T(8,128)} async-done(((f32[4,512,1,512]{3,1,2,0:T(8,128)}), f32[64,512,1,512]{3,1,2,0:T(8,128)}) %all-gather.8.cloned.1.call-update) | async-done | bytes 67108880 | tf_op jit(solution)/shard_map/all_gather | solution.py:9
  383.3 23.1 %reduce_sum.27 = f32[4,512,512]{2,1,0:T(8,128)} reduce(f32[16,4,512,512]{3,2,1,0:T(8,128)} %bitcast.1, f32[]{:T(128)} %constant.124.clone.1), dimensions={0}, to_apply=%region_0.1 | reduce | flops 15728640 | bytes 71303168 | tf_op jit(solution)/shard_map/reduce_sum | solution.py:9
  406.4 2.3 slice_select_fusion.1
  408.7 0.0 all-gather.6.cloned.1.call-update
  408.7 0.0 all-gather.10.cloned.1.call-start
  408.8 5.3 copy.41
  414.1 5.0 bitcast_select_fusion
  419.1 5.8 copy.39
  424.9 149.2 %all-gather.6.cloned.1.call-done = f32[8,512,512]{2,1,0:T(8,128)} async-done(((f32[1,512,512]{2,1,0:T(8,128)}), f32[8,512,512]{2,1,0:T(8,128)}) %all-gather.6.cloned.1.call-update) | async-done | bytes 8388624 | tf_op jit(solution)/shard_map/all_gather | solution.py:9
  574.1 4.5 reduce_sum.28
  578.6 0.0 copy-done
  578.6 0.0 copy-start.2
  578.6 3.5 fusion.32
  582.1 3.5 fusion.33
  585.5 0.0 copy-done.2
  585.6 0.0 copy-start.10
  585.6 8.2 fusion.28
  593.8 0.0 copy-start.6
  593.8 2.1 copy-done.6
  595.9 0.0 copy-done.10
  595.9 8.6 multiply_subtract_fusion
  604.5 0.0 copy-start.4
  604.5 4.5 pad_maximum_fusion
  609.0 0.0 copy-done.4
  609.0 4.6 constant_dynamic-slice_fusion
  613.6 5.4 copy.71
  619.0 2.8 broadcast_select_fusion
  621.7 0.0 all-gather.10.cloned.1.call-update
  621.8 0.3 copy.54
  622.1 643.2 %all-gather.10.cloned.1.call-done = f32[16,1,512,1024]{3,2,1,0:T(8,128)} async-done(((f32[2,1,512,1024]{3,2,1,0:T(8,128)}), f32[16,1,512,1024]{3,2,1,0:T(8,128)}) %all-gather.10.cloned.1.call-update) | async-done | bytes 33554448 | tf_op jit(solution)/shard_map/all_gather | solution.py:9
  1265.3 0.0 copy-start.3
  1265.3 13.0 bitcast_reduce_fusion
  1278.3 0.0 copy-start.8
  1278.3 1.9 copy-done.8
  1280.3 0.0 copy-done.3
  1280.3 0.0 copy-start.5
  1280.3 16.4 %fusion.3 = f32[4,512,2,512]{1,3,0,2:T(8,128)} fusion(f32[4,512,512]{1,2,0:T(8,128)S(1)} %copy-done.3, f32[2,512,1024]{2,1,0:T(8,128)S(1)} %bitcast_reduce_fusion), kind=kOutput, calls=%fused_computation.8 | convolution fusion | flops 12884901888 | bytes 14680064 | tf_op jit(solution)/shard_map/bik,cjk->bicj/dot_general | solution.py:47
  1296.6 0.0 copy-done.5
  1296.6 0.0 copy-start.7
  1296.6 20.6 %subtract_subtract_fusion = f32[4,512,2,512]{1,3,0,2:T(8,128)S(1)} fusion(f32[4,512,2,512]{1,3,0,2:T(8,128)} %fusion.3, f32[4,512,512]{1,2,0:T(8,128)S(1)} %copy-done.5, f32[2,512,1024]{2,1,0:T(8,128)} %copy-done.8, f32[4,1,512,2,1,512]{2,5,0,3,4,1:T(8,128)} %copy.37), kind=kOutput, calls=%fused_computation.2 | convolution fusion | flops 12889096192 | bytes 31457280 | tf_op jit(solution)/shard_map/bik,cjk->bicj/dot_general | solution.py:46
  1317.2 0.0 copy-done.7
  1317.2 2.2 fusion.2
  1319.4 0.0 copy-start.9
  1319.4 4.3 copy.77
  1323.6 1.0 copy-done.9
  1324.6 4.9 bitcast_dynamic-update-slice_fusion
  1329.5 1.2 fusion.26
  1330.7 0.0 copy-start.1
  1330.7 20.6 %copy.56 = f32[4,1,512,2,1,512]{5,4,3,2,1,0:T(1,128)} copy(f32[4,1,512,2,1,512]{2,5,0,3,4,1:T(8,128)} %fusion.26) | data formatting | bytes 16777216 | tf_op jit(solution)/shard_map/scatter | solution.py:54
  1351.3 0.0 copy-done.1
  (1 shorter events, 0.0 us)
Async XLA Ops:
  6.5 572.0 %copy-start = (f32[512,512]{1,0:T(8,128)S(1)}, f32[512,512]{1,0:T(8,128)}, u32[]{:S(2)}) copy-start(f32[512,512]{1,0:T(8,128)} %param.11) | copy-start | bytes 3145732
  6.5 376.8 %all-gather.8.cloned.1.call-start = ((), (), s32[]{:S(2)}) async-start(), calls=%async_computation.1 | async-start | bytes 71303168 | tf_op jit(solution)/shard_map/all_gather | solution.py:9
  37.1 537.0 %all-gather.6.cloned.1.call-start = ((), (), s32[]{:S(2)}) async-start(), calls=%async_computation | async-start | bytes 9437184 | tf_op jit(solution)/shard_map/all_gather | solution.py:9
  408.7 856.6 %all-gather.10.cloned.1.call-start = ((), (), s32[]{:S(2)}) async-start(), calls=%async_computation.2 | async-start | bytes 37748736 | tf_op jit(solution)/shard_map/all_gather | solution.py:9
  578.6 7.0 copy-start.2
  585.6 10.3 copy-start.10
  593.8 2.1 copy-start.6
  604.5 4.5 copy-start.4
  1265.3 14.9 %copy-start.3 = (f32[4,512,512]{1,2,0:T(8,128)S(1)}, f32[4,512,512]{1,2,0:T(8,128)}, u32[]{:S(2)}) copy-start(f32[4,512,512]{1,2,0:T(8,128)} %bitcast_select_fusion) | copy-start | bytes 12582916
  1278.3 2.0 copy-start.8
  1280.3 16.4 %copy-start.5 = (f32[4,512,512]{1,2,0:T(8,128)S(1)}, f32[4,512,512]{1,2,0:T(8,128)}, u32[]{:S(2)}) copy-start(f32[4,512,512]{1,2,0:T(8,128)} %copy-done.4) | copy-start | bytes 12582916
  1296.6 20.6 %copy-start.7 = (f32[4,512,512]{1,2,0:T(8,128)S(1)}, f32[4,512,512]{1,2,0:T(8,128)}, u32[]{:S(2)}) copy-start(f32[4,512,512]{1,2,0:T(8,128)} %copy-done.6) | copy-start | bytes 12582916
  1319.4 5.2 copy-start.9
  1330.7 20.6 %copy-start.1 = (f32[512,512]{1,0:T(8,128)S(1)}, f32[512,512]{1,0:T(8,128)}, u32[]{:S(2)}) copy-start(f32[512,512]{1,0:T(8,128)} %param.11) | copy-start | bytes 3145732
Sparse Core Ops, SparseCore 0:
  37.2 346.0 all-gather.7
  408.9 165.1 all-gather.5
  621.9 643.3 all-gather.9
